TPU v7x, 32 devices: a whole 2x2x4 slice. The times are simulated.
32 devices in a mesh: bin: 4 (over x, core), slab: 8 (over z, y).
Axes of the slice: x: 2, y: 2, z: 4, core: 2. Of those that a mesh axis runs over, the one named last changes fastest.
Arguments:
- volumes: float32 [8, 32, 64, 512], P('bin', 'slab'), may hold values from -6 to 6
- attenuation: float32 [8, 3], replicated, may hold values from 0.2 to 1.2
- penalty: float32 [1], replicated, may hold values from 0.2 to 0.4
- tv_weight: float32 [1], replicated, may hold values from 0.3 to 0.8
Outputs:
- materials: float32 [3, 32, 64, 512], P(None, ('bin', 'slab'))
All inputs are finite; a program needn't handle non-finite values.
Results may differ from a plain program's by a relative error of at most 0.0001.
Values sent between devices are 32-bit elements; how exact they have to be, the bound alone decides.
No kernel may reach another device: no remote copies, remote signals or barrier semaphores. Data moves between devices by JAX's collectives and lax.ppermute only.
A program may use at most 64 MiB of HBM per device.

v0:
```python
import functools
import math

import jax
import jax.numpy as jnp
from jax import lax
from jax.experimental import pallas as pl
from jax.experimental.pallas import tpu as pltpu
from jax.sharding import PartitionSpec as P


ITERS = 3
EDGE = 4
GRANT = 56_000 * 1024
ROUNDS = (1, 3, 0, 2)
TWISTS = 32770
VMEM = pltpu.VMEM


def window_start(quarter, rows, total):
    return min(max(rows * quarter - EDGE, 0), total - rows - 2 * EDGE)


def inverse_three(m):
    cof = [
        [
            m[(r + 1) % 3][(c + 1) % 3] * m[(r + 2) % 3][(c + 2) % 3]
            - m[(r + 1) % 3][(c + 2) % 3] * m[(r + 2) % 3][(c + 1) % 3]
            for c in range(3)
        ]
        for r in range(3)
    ]
    det = m[0][0] * cof[0][0] + m[0][1] * cof[0][1] + m[0][2] * cof[0][2]
    over = 1.0 / det
    return [[cof[c][r] * over for c in range(3)] for r in range(3)]


def away_kernel(volumes, first, second, sem):
    c = lax.axis_index("bin") % 2
    copies = [
        pltpu.make_async_copy(volumes.at[k, 2 * (1 - c) + e], ref.at[k], sem.at[e, k])
        for e, ref in enumerate((first, second))
        for k in range(2)
    ]
    for copy in copies:
        copy.start()
    for copy in copies:
        copy.wait()


def spread(x):
    return jnp.broadcast_to(x, (8, 128))


def ready_kernel(bins, pen, tvw, att, numbers):
    a = [[att[bins * m + k] for k in range(bins)] for m in range(3)]
    pen_value = spread(pen[...].reshape(1, 1))
    gram = [[None] * 3 for _ in range(3)]
    for i in range(3):
        for j in range(i, 3):
            total = a[i][0] * a[j][0]
            for k in range(1, bins):
                total = total + a[i][k] * a[j][k]
            gram[i][j] = gram[j][i] = total
    for i in range(3):
        gram[i][i] = gram[i][i] + 12.0 * pen_value
    inv = inverse_three(gram)
    for m in range(3):
        for n in range(3):
            numbers[3 * m + n] = inv[m][n]
            numbers[9 + 3 * m + n] = pen_value * inv[m][n]
    numbers[18] = spread(tvw[...].reshape(1, 1)) / pen_value


def project_kernel(dims, e, att, volumes, other, own, to_x, to_y, to_xy, part):
    bins, rows, total, lanes, _ = dims
    c, me, _ = place()
    b = lax.axis_index("bin")
    a = [[att[bins * m + k] for k in range(bins)] for m in range(3)]
    w = []
    for k in range(4):
        group = b if k < 2 else b ^ 1
        row = []
        for m in range(3):
            value = a[m][k % 2]
            for g in range(1, bins // 2):
                value = jnp.where(group == g, a[m][2 * g + k % 2], value)
            row.append(value)
        w.append(row)

    def body(t, carry):
        tile = pl.ds(pl.multiple_of(t * 8, 8), 8)
        for col in range(lanes // 128):
            at = (tile, slice(128 * col, 128 * col + 128))
            v = [volumes[(0, 2 * c + e, *at)], volumes[(1, 2 * c + e, *at)], other[(0, *at)], other[(1, *at)]]
            for m in range(3):
                part[(m, *at)] = v[0] * w[0][m] + v[1] * w[1][m] + (v[2] * w[2][m] + v[3] * w[3][m])
        return carry

    lax.fori_loop(0, total // 8, body, 0)
    width = rows + 2 * EDGE
    for rel, ref in enumerate((own, to_y, to_x, to_xy)):
        for quarter in range(4):

            @pl.when((me ^ rel) == quarter)
            def _(ref=ref, quarter=quarter):
                start = window_start(quarter, rows, total)
                ref[...] = part[:, start : start + width, :]


def sum_kernel(dims, numbers, *refs):
    parts, (f0, far, near, cross) = (refs[:4], refs[4:8]), refs[8:]
    y = lax.axis_index("slab") % 2
    c = lax.axis_index("bin") % 2
    _, rows, _, lanes, _ = dims
    inv = [[numbers[3 * m + n] for n in range(3)] for m in range(3)]
    for e in range(2):
        own, from_x, from_y, from_xy = parts[e]
        for to, one, two in ((3 + 4 * y, own, from_x), (7 - 4 * y, from_y, from_xy)):
            for t in range((rows + 2 * EDGE) // 8):
                for col in range(lanes // 128):
                    at = (slice(8 * t, 8 * t + 8), slice(128 * col, 128 * col + 128))
                    d = [one[(m, *at)] + two[(m, *at)] for m in range(3)]
                    for m in range(3):
                        f0[(m, to - 2 * c + e, *at)] = inv[m][0] * d[0] + inv[m][1] * d[1] + inv[m][2] * d[2]
    for core in range(2):

        @pl.when(c == core)
        def _(core=core):
            slab = [f0.at[:, 3 + 4 * k - 2 * core + e] for k in range(2) for e in range(2)]
            far[:, 0] = slab[2 * core][...]
            far[:, 1] = slab[2 * core + 1][...]
            near[:, 0] = slab[2 * (1 - core) + 1 - core][...]
            for at, k in enumerate(((1, 2, 3), (0, 1, 2))[core]):
                cross[:, at] = slab[k][...]


def place():
    b = lax.axis_index("bin")
    s = lax.axis_index("slab")
    c = b % 2
    return c, 2 * (b // 2) + s % 2, (s // 2) * 8 + 4 * c - 3


def layer_stepper(dims, numbers, fields, dual, down):
    _, rows, _, lanes, depth = dims
    tiles, columns = (rows + 2 * EDGE) // 8, lanes // 128
    _, me, z_base = place()
    inv = [[numbers[9 + 3 * m + n] for n in range(3)] for m in range(3)]
    twice = [[numbers[9 + 3 * m + n] + numbers[9 + 3 * m + n] for n in range(3)] for m in range(3)]
    threshold = numbers[18]
    squared = threshold * threshold
    lane = lax.broadcasted_iota(jnp.int32, (8, 128), 1)
    sub = lax.broadcasted_iota(jnp.int32, (8, 128), 0)
    last_lane, first_lane = lane == 127, lane == 0
    last_sub, first_sub = sub == 7, sub == 0
    at_end = last_sub & (me == 3)
    zero = jnp.zeros((8, 128), jnp.float32)

    def at(t, col):
        return slice(8 * t, 8 * t + 8), slice(128 * col, 128 * col + 128)

    def layer_step(i, turn):
        src, dst, first = fields[turn], fields[turn + 1], fields[0]
        final = turn == ITERS - 1
        to = i - 2 if final else i
        by = twice if turn == 0 else inv
        z = z_base + i
        above = jnp.where((z >= 0) & (z < depth - 1), i + 1, i)

        def load(ref, m, layer, t, col):
            return ref[(m, layer) + at(t, col)]

        belows = [None] * columns
        for t in range(tiles):
            before = None
            f = [load(src, m, i, t, 0) for m in range(3)]
            f_rolled = [pltpu.roll(f[m], 127, 1) for m in range(3)]
            for col in range(columns):
                following = None
                if t + 1 < tiles:
                    following = [load(src, m, i, t + 1, col) for m in range(3)]
                f_next = f_next_rolled = None
                if col + 1 < columns:
                    f_next = [load(src, m, i, t, col + 1) for m in range(3)]
                    f_next_rolled = [pltpu.roll(f_next[m], 127, 1) for m in range(3)]
                below = belows[col]
                v = []
                for m in range(3):
                    gz = load(src, m, above, t, col) - f[m]
                    up = pltpu.roll(f[m], 7, 0)
                    if following is not None:
                        up = jnp.where(last_sub, pltpu.roll(following[m], 7, 0), up)
                    else:
                        up = jnp.where(at_end, f[m], up)
                    nxt = f[m] if f_next is None else f_next_rolled[m]
                    ahead = jnp.where(last_lane, nxt, f_rolled[m])
                    v.append([gz, up - f[m], ahead - f[m]])
                old = None
                if turn > 0:
                    old = [[load(dual, 3 * m + d, i, t, col) for d in range(3)] for m in range(3)]
                    v = [[v[m][d] + old[m][d] for d in range(3)] for m in range(3)]
                squares = [v[m][0] * v[m][0] + v[m][1] * v[m][1] + v[m][2] * v[m][2] for m in range(3)]
                scale = threshold * lax.rsqrt(jnp.maximum(squares[0] + squares[1] + squares[2], squared))
                if final:
                    scale = scale + scale
                fresh = [[v[m][d] * scale for d in range(3)] for m in range(3)]
                if not final:
                    for m in range(3):
                        for d in range(3):
                            dual[(3 * m + d, i) + at(t, col)] = fresh[m][d]
                if turn == 0:
                    step = fresh
                elif final:
                    step = [[fresh[m][d] - old[m][d] for d in range(3)] for m in range(3)]
                else:
                    step = [[(fresh[m][d] + fresh[m][d]) - old[m][d] for d in range(3)] for m in range(3)]
                lower = [down[(m,) + at(t, col)] for m in range(3)]
                for m in range(3):
                    down[(m,) + at(t, col)] = step[m][0]
                rolled_y = [pltpu.roll(step[m][1], 1, 0) for m in range(3)]
                rolled_x = [pltpu.roll(step[m][2], 1, 1) for m in range(3)]
                rhs = []
                for m in range(3):
                    prev_y = jnp.where(first_sub, zero if below is None else below[m], rolled_y[m])
                    prev_x = jnp.where(first_lane, zero if before is None else before[m], rolled_x[m])
                    div = (step[m][0] - lower[m]) + (step[m][1] - prev_y) + (step[m][2] - prev_x)
                    rhs.append((6.0 if turn == 0 else 12.0) * f[m] + div)
                belows[col], before = rolled_y, rolled_x
                for m in range(3):
                    dst[(m, to) + at(t, col)] = load(first, m, i, t, col) + (
                        by[m][0] * rhs[0] + by[m][1] * rhs[1] + by[m][2] * rhs[2]
                    )
                f, f_rolled = f_next, f_next_rolled

    def run(start, count, turn):
        def body(i, carry):
            layer_step(start + i, turn)
            return carry

        lax.fori_loop(0, count, body, 0)

    def correct(i, turn):
        dst = fields[turn + 1]
        by = twice if turn == 0 else inv
        to = i - 2 if turn == ITERS - 1 else i
        for col in range(columns):
            for t in range(tiles):
                low = [down[(m,) + at(t, col)] for m in range(3)]
                for m in range(3):
                    dst[(m, to) + at(t, col)] = dst[(m, to) + at(t, col)] - (
                        by[m][0] * low[0] + by[m][1] * low[1] + by[m][2] * low[2]
                    )

    return run, correct


def inner_kernel(dims, numbers, cross, held, f0, f1, f2, f3, dual, kept, down):
    c, _, _ = place()
    for core in range(2):

        @pl.when(c == core)
        def _(core=core):
            for k, to in enumerate(((5, 6, 9), (0, 3, 4))[core]):
                f0[:, to] = cross[:, k]

    run, _ = layer_stepper(dims, numbers, (f0, f1, f2, f3), dual, down)
    for turn in range(ITERS):
        down[...] = jnp.zeros_like(down)
        run(jnp.where(c == 0, 3, 0) + turn, 6 - 2 * turn, turn)
        kept[turn] = down[...]


def outer_kernel(dims, numbers, far, near, g0, g1, g2, g3, gd, kept, f0, f1, f2, f3, dual, o0, o1, o2, o3, down):
    _, rows, total, _, _ = dims
    c, me, _ = place()
    for core in range(2):

        @pl.when(c == core)
        def _(core=core):
            for k, to in enumerate(((1, 2, 0), (7, 8, 9))[core]):
                f0[:, to] = far[:, k] if k < 2 else near[:, 0]

    run, correct = layer_stepper(dims, numbers, (f0, f1, f2, f3), dual, down)
    for turn in range(ITERS):

        @pl.when(c == 0)
        def _():
            down[...] = jnp.zeros_like(down)

        @pl.when(c == 1)
        def _(turn=turn):
            down[...] = kept[turn]

        run(jnp.where(c == 0, turn, 6 - turn), 3, turn)

        @pl.when(c == 0)
        def _(turn=turn):
            correct(3 + turn, turn)

    twist = twist_of(c, lax.axis_index("slab") // 2, lax.axis_size("slab"))
    for quarter in range(4):

        @pl.when(me == quarter)
        def _(quarter=quarter):
            start = rows * quarter - window_start(quarter, rows, total)
            for key, out in zip(ROUNDS, (o0, o1, o2, o3)):
                out[...] = f3[:, 1 + (key ^ quarter ^ twist), start : start + rows, :]


def twist_of(core, plane, slabs):
    return (TWISTS >> (2 * (4 * core + plane // (slabs // 8)))) & 3


def gather_kernel(rows, r0, r1, r2, r3, out, sem):
    slabs = lax.axis_size("slab")
    z = lax.axis_index("bin") * slabs + lax.axis_index("slab")
    twist = twist_of(z // 4 % 2, z // 8, slabs)
    copies = []
    for n, (t, ref) in enumerate(zip(ROUNDS, (r0, r1, r2, r3))):
        at = pl.multiple_of((z % 4 ^ t ^ twist) * rows, 8)
        copies.append(pltpu.make_async_copy(ref, out.at[:, 0, pl.ds(at, rows), :], sem.at[n]))
        copies[-1].start()
    for copy in copies:
        copy.wait()


def call(kernel, outs, args, spaces=None, scratch=(), aliases=None, flops=0, out_space=VMEM, limit=None):
    shapes = [jax.ShapeDtypeStruct(o, jnp.float32) for o in outs]
    spaces = spaces or [VMEM] * len(args)
    held = sum(math.prod(a.shape) for a in (*shapes, *args, *scratch))
    return pl.pallas_call(
        kernel,
        out_shape=shapes,
        in_specs=[pl.BlockSpec(memory_space=m) for m in spaces],
        out_specs=[pl.BlockSpec(memory_space=m) for m in [out_space] * len(outs)],
        scratch_shapes=list(scratch),
        input_output_aliases=aliases or {},
        cost_estimate=pl.CostEstimate(flops=flops, bytes_accessed=4 * held, transcendentals=0),
        compiler_params=pltpu.CompilerParams(vmem_limit_bytes=limit or 4 * held + (2 << 20)),
    )(*args)


def on_device(mesh_bin, mesh_slab, volumes, attenuation, penalty, tv_weight):
    own_bins, layers, total, lanes = volumes.shape
    bins = own_bins * mesh_bin
    assert mesh_bin == 4 and own_bins == 2 and layers == 4 and mesh_slab % 4 == 0
    rows = total // 4
    width = rows + 2 * EDGE
    depth = layers * mesh_slab
    devices = [(b, s) for b in range(mesh_bin) for s in range(mesh_slab)]

    def send(x, where):
        pairs = []
        for b, s in devices:
            to = where(b, s)
            if 0 <= to[0] < mesh_bin and 0 <= to[1] < mesh_slab:
                pairs.append((b * mesh_slab + s, to[0] * mesh_slab + to[1]))
        return lax.ppermute(x, ("bin", "slab"), pairs)

    dims = (bins, rows, total, lanes, depth)
    spreads = jnp.broadcast_to(attenuation.T.reshape(3 * bins, 1, 1), (3 * bins, 8, 128))
    away = call(
        away_kernel,
        [(2, total, lanes)] * 2,
        (volumes,),
        [pl.ANY],
        [pltpu.SemaphoreType.DMA((2, 2))],
        limit=GRANT - 6 * 2 * total * lanes * 4,
    )
    others = [send(part, lambda b, s: (b ^ 1, s)) for part in away]
    win = (3, 2, width, lanes)
    parts = []
    for e, other in enumerate(others):
        own, to_x, to_y, to_xy = call(
            functools.partial(project_kernel, dims, e),
            [(3, width, lanes)] * 4,
            (spreads, volumes, other),
            scratch=[VMEM((3, total, lanes), jnp.float32)],
        )
        from_xy = send(to_xy, lambda b, s: (b ^ 2, s ^ 1))
        from_x = send(to_x, lambda b, s: (b ^ 2, s))
        from_y = send(to_y, lambda b, s: (b, s ^ 1))
        parts += [own, from_x, from_y, from_xy]
    numbers = call(
        functools.partial(ready_kernel, bins), [(19, 8, 128)], (penalty, tv_weight, spreads)
    )[0]
    state = [(3, 10, width, lanes)] * 3 + [(3, 5, width, lanes), (9, 9, width, lanes)]
    f0, far, near, cross = call(
        functools.partial(sum_kernel, dims),
        [state[0], win, (3, 1, width, lanes), (3, 3, width, lanes)],
        (numbers, *parts),
    )
    far = send(far, lambda b, s: (b ^ 1, s + (2 if b % 2 else -2)))
    near = send(near, lambda b, s: (b, s + (-2 if b % 2 else 2)))
    cross = send(cross, lambda b, s: (b ^ 1, s))
    work = 150 * width * lanes
    scratch = [VMEM((3, width, lanes), jnp.float32)]
    inner = call(
        functools.partial(inner_kernel, dims),
        state + [(3, 3, width, lanes)],
        (numbers, cross, f0),
        None,
        scratch,
        {2: 0},
        12 * work,
    )
    blocks = call(
        functools.partial(outer_kernel, dims),
        state + [(3, rows, lanes)] * 4,
        (numbers, far, near, *inner),
        None,
        scratch,
        {3 + i: i for i in range(5)},
        9 * work,
    )[5:]

    def owner(t):
        def where(b, s):
            j = t ^ (2 * (b // 2) + s % 2) ^ twist_of(b % 2, s // 2, mesh_slab)
            z = (s // 2) * 8 + 4 * (b % 2) + j
            return z // mesh_slab, z % mesh_slab

        return where

    blocks = [send(block, owner(key)) for key, block in zip(ROUNDS, blocks)]
    return call(
        functools.partial(gather_kernel, rows),
        [(3, 1, total, lanes)],
        blocks,
        scratch=[pltpu.SemaphoreType.DMA((4,))],
        out_space=pl.ANY,
    )[0]


def solution(mesh):
    placed = (P("bin", "slab", None, None), P(), P(), P())
    return jax.shard_map(
        functools.partial(on_device, mesh.shape["bin"], mesh.shape["slab"]),
        mesh=mesh,
        in_specs=placed,
        out_specs=P(None, ("bin", "slab"), None, None),
        check_vma=False,
    )
```

profile of v0, /device:TPU:7, one launch (start us, length us, event | category | flops | bytes accessed | tf_op | source)
XLA Modules:
  0.0 47.9 jit_solution(7463530778906948526)
XLA Ops:
  0.0 1.2 %shard_map.47 = (f32[2,64,512]{2,1,0:T(8,128)S(1)}, f32[2,64,512]{2,1,0:T(8,128)S(1)}) custom-call(f32[2,4,64,512]{3,2,1,0:T(8,128)} %volumes.5), custom_call_target="tpu_custom_call" | custom-call | bytes 1572880 | tf_op jit(solution)/shard_map/pallas_call | solution.py:332
  1.2 0.7 %collective-permute-start.4 = (f32[2,64,512]{2,1,0:T(8,128)S(1)}, f32[2,64,512]{2,1,0:T(8,128)S(1)}, u32[]{:S(2)}, u32[]{:S(2)}) collective-permute-start(f32[2,64,512]{2,1,0:T(8,128)S(1)} %get-tuple-element.34), channel_id=1, source_target_pairs={{0,8},{1,9},{2,10},{3,11},{4,12},{5,13},{6,14},{7,15},{8,0},{9,1},... | collective-permute-start | bytes 786440 | tf_op jit(solution)/shard_map/ppermute | solution.py:359
  2.0 0.8 %broadcast_in_dim.7 = f32[24]{0:T(128)S(1)} reshape(f32[3,8]{1,0:T(4,128)} %bitcast.1) | data formatting | bytes 192 | tf_op jit(solution)/shard_map/broadcast_in_dim | solution.py:362
  2.8 0.3 collective-permute-done.4.other
  3.5 0.3 collective-permute-start.5
  3.9 2.3 %collective-permute-start.7 = (f32[3,24,512]{2,1,0:T(8,128)S(1)}, f32[3,24,512]{2,1,0:T(8,128)S(1)}, u32[]{:S(2)}, u32[]{:S(2)}) collective-permute-start(f32[3,24,512]{2,1,0:T(8,128)S(1)} %get-tuple-element.38), channel_id=1, source_target_pairs={{0,17},{1,16},{2,19},{3,18},{4,21},{5,20},{6,23},{7,22},{8,25},{9,... | collective-permute-start | bytes 442376 | tf_op jit(solution)/shard_map/ppermute | solution.py:359
  6.9 1.7 %collective-permute-done.5.refs_5_ = f32[3,24,512]{2,1,0:T(8,128)S(1)} collective-permute-done((f32[3,24,512]{2,1,0:T(8,128)S(1)}, f32[3,24,512]{2,1,0:T(8,128)S(1)}, u32[]{:S(2)}, u32[]{:S(2)}) %collective-permute-start.5) | collective-permute-done | bytes 147488 | tf_op jit(solution)/shard_map/ppermute | solution.py:359
  8.6 0.6 %collective-permute-start.3 = (f32[3,24,512]{2,1,0:T(8,128)S(1)}, f32[3,24,512]{2,1,0:T(8,128)S(1)}, u32[]{:S(2)}, u32[]{:S(2)}) collective-permute-start(f32[3,24,512]{2,1,0:T(8,128)S(1)} %get-tuple-element.33), channel_id=1, source_target_pairs={{0,17},{1,16},{2,19},{3,18},{4,21},{5,20},{6,23},{7,22},{8,25},{9,... | collective-permute-start | bytes 442376 | tf_op jit(solution)/shard_map/ppermute | solution.py:359
  10.6 1.1 %collective-permute-done.7.refs_7_ = f32[3,24,512]{2,1,0:T(8,128)S(1)} collective-permute-done((f32[3,24,512]{2,1,0:T(8,128)S(1)}, f32[3,24,512]{2,1,0:T(8,128)S(1)}, u32[]{:S(2)}, u32[]{:S(2)}) %collective-permute-start.7) | collective-permute-done | bytes 147488 | tf_op jit(solution)/shard_map/ppermute | solution.py:359
  11.8 3.2 %collective-permute-done.1.refs_1_ = f32[3,24,512]{2,1,0:T(8,128)S(1)} collective-permute-done((f32[3,24,512]{2,1,0:T(8,128)S(1)}, f32[3,24,512]{2,1,0:T(8,128)S(1)}, u32[]{:S(2)}, u32[]{:S(2)}) %collective-permute-start.1) | collective-permute-done | bytes 147488 | tf_op jit(solution)/shard_map/ppermute | solution.py:359
  15.0 0.8 %collective-permute-done.2.refs_2_ = f32[3,24,512]{2,1,0:T(8,128)S(1)} collective-permute-done((f32[3,24,512]{2,1,0:T(8,128)S(1)}, f32[3,24,512]{2,1,0:T(8,128)S(1)}, u32[]{:S(2)}, u32[]{:S(2)}) %collective-permute-start.2) | collective-permute-done | bytes 147488 | tf_op jit(solution)/shard_map/ppermute | solution.py:359
  15.8 2.3 %collective-permute-done.3.refs_3_ = f32[3,24,512]{2,1,0:T(8,128)S(1)} collective-permute-done((f32[3,24,512]{2,1,0:T(8,128)S(1)}, f32[3,24,512]{2,1,0:T(8,128)S(1)}, u32[]{:S(2)}, u32[]{:S(2)}) %collective-permute-start.3) | collective-permute-done | bytes 147488 | tf_op jit(solution)/shard_map/ppermute | solution.py:359
  18.3 1.5 %collective-permute-start.10 = (f32[3,3,24,512]{3,2,1,0:T(8,128)S(1)}, f32[3,3,24,512]{3,2,1,0:T(8,128)S(1)}, u32[]{:S(2)}, u32[]{:S(2)}) collective-permute-start(f32[3,3,24,512]{3,2,1,0:T(8,128)S(1)} %get-tuple-element.41), channel_id=1, source_target_pairs={{0,8},{1,9},{2,10},{3,11},{4,12},{5,13},{6,14},{7,15},{8,0},{9,1},... | collective-permute-start | bytes 1327112 | tf_op jit(solution)/shard_map/ppermute | solution.py:359
  19.8 3.1 %collective-permute-start.8 = (f32[3,2,24,512]{3,2,1,0:T(8,128)S(1)}, f32[3,2,24,512]{3,2,1,0:T(8,128)S(1)}, u32[]{:S(2)}, u32[]{:S(2)}) collective-permute-start(f32[3,2,24,512]{3,2,1,0:T(8,128)S(1)} %get-tuple-element.39), channel_id=1, source_target_pairs={{2,8},{3,9},{4,10},{5,11},{6,12},{7,13},{8,2},{9,3},{10,4},{11,5},... | collective-permute-start | bytes 884744 | tf_op jit(solution)/shard_map/ppermute | solution.py:359
  22.9 1.3 %collective-permute-start.9 = (f32[3,1,24,512]{3,2,1,0:T(8,128)S(1)}, f32[3,1,24,512]{3,2,1,0:T(8,128)S(1)}, u32[]{:S(2)}, u32[]{:S(2)}) collective-permute-start(f32[3,1,24,512]{3,2,1,0:T(8,128)S(1)} %get-tuple-element.40), channel_id=1, source_target_pairs={{0,2},{1,3},{2,4},{3,5},{4,6},{5,7},{10,8},{11,9},{12,10},{13,11},... | collective-permute-start | bytes 442376 | tf_op jit(solution)/shard_map/ppermute | solution.py:359
  24.3 3.1 %shard_map.51 = (f32[3,10,24,512]{3,2,1,0:T(8,128)S(1)}, f32[3,10,24,512]{3,2,1,0:T(8,128)S(1)}, f32[3,10,24,512]{3,2,1,0:T(8,128)S(1)}, f32[3,5,24,512]{3,2,1,0...) custom-call(f32[19,8,128]{2,1,0:T(8,128)S(1)} %shard_map.46.numbers, ...), custom_call_target="tpu_custom_call", output_to_operand_aliasing={{0}: (2, {})} | custom-call | flops 22118400 | bytes 11726848 | tf_op jit(solution)/shard_map/pallas_call | solution.py:332
  27.4 2.1 %collective-permute-done.9.near = f32[3,1,24,512]{3,2,1,0:T(8,128)S(1)} collective-permute-done((f32[3,1,24,512]{3,2,1,0:T(8,128)S(1)}, f32[3,1,24,512]{3,2,1,0:T(8,128)S(1)}, u32[]{:S(2)}, u32[]{:S(2)}) %collective-permute-start.9) | collective-permute-done | bytes 147488 | tf_op jit(solution)/shard_map/ppermute | solution.py:359
  29.4 2.4 %shard_map.52 = (f32[3,10,24,512]{3,2,1,0:T(8,128)S(1)}, f32[3,10,24,512]{3,2,1,0:T(8,128)S(1)}, f32[3,10,24,512]{3,2,1,0:T(8,128)S(1)}, f32[3,5,24,512]{3,2,1,0...) custom-call(f32[19,8,128]{2,1,0:T(8,128)S(1)} %shard_map.46.numbers,, ...), custom_call_target="tpu_custom_call", output_to_operand_aliasing={{0}: (3, {}), {1}: (4, {}), {2}: (5, {}), {3}: (6, {}), {4}... | custom-call | flops 16588800 | bytes 19787776 | tf_op jit(solution)/shard_map/pallas_call | solution.py:332
  31.9 4.3 %collective-permute-start.11 = (f32[3,16,512]{2,1,0:T(8,128)S(1)}, f32[3,16,512]{2,1,0:T(8,128)S(1)}, u32[]{:S(2)}, u32[]{:S(2)}) collective-permute-start(f32[3,16,512]{2,1,0:T(8,128)S(1)} %get-tuple-element.49), channel_id=1, source_target_pairs={{0,3},{1,2},{2,9},{3,8},{4,17},{5,16},{6,25},{7,24},{8,5},{9,4},{1... | collective-permute-start | bytes 294920 | tf_op jit(solution)/shard_map/ppermute | solution.py:359
  36.1 3.3 %collective-permute-start.13 = (f32[3,16,512]{2,1,0:T(8,128)S(1)}, f32[3,16,512]{2,1,0:T(8,128)S(1)}, u32[]{:S(2)}, u32[]{:S(2)}) collective-permute-start(f32[3,16,512]{2,1,0:T(8,128)S(1)} %get-tuple-element.51), channel_id=1, source_target_pairs={{0,2},{1,3},{2,8},{3,9},{4,16},{5,17},{6,24},{7,25},{8,4},{9,5},{1... | collective-permute-start | bytes 294920 | tf_op jit(solution)/shard_map/ppermute | solution.py:359
  39.4 1.9 %collective-permute-start.14 = (f32[3,16,512]{2,1,0:T(8,128)S(1)}, f32[3,16,512]{2,1,0:T(8,128)S(1)}, u32[]{:S(2)}, u32[]{:S(2)}) collective-permute-start(f32[3,16,512]{2,1,0:T(8,128)S(1)} %get-tuple-element.52), channel_id=1, source_target_pairs={{0,0},{1,1},{2,10},{3,11},{4,18},{5,19},{6,26},{7,27},{8,6},{9,7},... | collective-permute-start | bytes 294920 | tf_op jit(solution)/shard_map/ppermute | solution.py:359
  41.3 1.6 %collective-permute-done.12.r1 = f32[3,16,512]{2,1,0:T(8,128)S(1)} collective-permute-done((f32[3,16,512]{2,1,0:T(8,128)S(1)}, f32[3,16,512]{2,1,0:T(8,128)S(1)}, u32[]{:S(2)}, u32[]{:S(2)}) %collective-permute-start.12) | collective-permute-done | bytes 98336 | tf_op jit(solution)/shard_map/ppermute | solution.py:359
  42.9 4.2 %collective-permute-done.14.r3 = f32[3,16,512]{2,1,0:T(8,128)S(1)} collective-permute-done((f32[3,16,512]{2,1,0:T(8,128)S(1)}, f32[3,16,512]{2,1,0:T(8,128)S(1)}, u32[]{:S(2)}, u32[]{:S(2)}) %collective-permute-start.14) | collective-permute-done | bytes 98336 | tf_op jit(solution)/shard_map/ppermute | solution.py:359
  47.1 0.8 %shard_map.53 = f32[3,1,64,512]{3,2,1,0:T(8,128)} custom-call(f32[3,16,512]{2,1,0:T(8,128)S(1)} %collective-permute-done.11.r0, f32[3,16,512]{2,1,0:T(8,128)S(1)} %collective-permute-done.12.r1, f32[3,16,512]{2,1,0:T(8,128)S(1)} %collective-permute-done.13.r2, f32[3,16,512]{2,1,0:T(8,128)S(1)} %collective-permute-done.14.r3), custom_call_target="tpu_custom_call" | custom-call | bytes 786448 | tf_op jit(solution)/shard_map/pallas_call | solution.py:332
  (18 shorter events, 1.4 us)
Async XLA Ops:
  0.0 3.2 %copy-start = (f32[2,4,64,512]{3,2,1,0:T(8,128)S(1)}, f32[2,4,64,512]{3,2,1,0:T(8,128)}, u32[]{:S(2)}) copy-start(f32[2,4,64,512]{3,2,1,0:T(8,128)} %volumes.5) | copy-start | bytes 3145732
  1.2 1.9 %collective-permute-start.4 = (f32[2,64,512]{2,1,0:T(8,128)S(1)}, f32[2,64,512]{2,1,0:T(8,128)S(1)}, u32[]{:S(2)}, u32[]{:S(2)}) collective-permute-start(f32[2,64,512]{2,1,0:T(8,128)S(1)} %get-tuple-element.34), channel_id=1, source_target_pairs={{0,8},{1,9},{2,10},{3,11},{4,12},{5,13},{6,14},{7,15},{8,0},{9,1},... | collective-permute-start | bytes 786440 | tf_op jit(solution)/shard_map/ppermute | solution.py:359
  2.0 4.3 %collective-permute-start = (f32[2,64,512]{2,1,0:T(8,128)S(1)}, f32[2,64,512]{2,1,0:T(8,128)S(1)}, u32[]{:S(2)}, u32[]{:S(2)}) collective-permute-start(f32[2,64,512]{2,1,0:T(8,128)S(1)} %get-tuple-element.29), channel_id=1, source_target_pairs={{0,8},{1,9},{2,10},{3,11},{4,12},{5,13},{6,14},{7,15},{8,0},{9,1},... | collective-permute-start | bytes 786440 | tf_op jit(solution)/shard_map/ppermute | solution.py:359
  3.5 5.1 %collective-permute-start.5 = (f32[3,24,512]{2,1,0:T(8,128)S(1)}, f32[3,24,512]{2,1,0:T(8,128)S(1)}, u32[]{:S(2)}, u32[]{:S(2)}) collective-permute-start(f32[3,24,512]{2,1,0:T(8,128)S(1)} %get-tuple-element.36), channel_id=1, source_target_pairs={{0,16},{1,17},{2,18},{3,19},{4,20},{5,21},{6,22},{7,23},{8,24},{9,... | collective-permute-start | bytes 442376 | tf_op jit(solution)/shard_map/ppermute | solution.py:359
  3.8 6.8 %collective-permute-start.6 = (f32[3,24,512]{2,1,0:T(8,128)S(1)}, f32[3,24,512]{2,1,0:T(8,128)S(1)}, u32[]{:S(2)}, u32[]{:S(2)}) collective-permute-start(f32[3,24,512]{2,1,0:T(8,128)S(1)} %get-tuple-element.37), channel_id=1, source_target_pairs={{0,1},{1,0},{2,3},{3,2},{4,5},{5,4},{6,7},{7,6},{8,9},{9,8},{10,11... | collective-permute-start | bytes 442376 | tf_op jit(solution)/shard_map/ppermute | solution.py:359
  3.9 7.9 %collective-permute-start.7 = (f32[3,24,512]{2,1,0:T(8,128)S(1)}, f32[3,24,512]{2,1,0:T(8,128)S(1)}, u32[]{:S(2)}, u32[]{:S(2)}) collective-permute-start(f32[3,24,512]{2,1,0:T(8,128)S(1)} %get-tuple-element.38), channel_id=1, source_target_pairs={{0,17},{1,16},{2,19},{3,18},{4,21},{5,20},{6,23},{7,22},{8,25},{9,... | collective-permute-start | bytes 442376 | tf_op jit(solution)/shard_map/ppermute | solution.py:359
  6.5 8.5 %collective-permute-start.1 = (f32[3,24,512]{2,1,0:T(8,128)S(1)}, f32[3,24,512]{2,1,0:T(8,128)S(1)}, u32[]{:S(2)}, u32[]{:S(2)}) collective-permute-start(f32[3,24,512]{2,1,0:T(8,128)S(1)} %get-tuple-element.31), channel_id=1, source_target_pairs={{0,16},{1,17},{2,18},{3,19},{4,20},{5,21},{6,22},{7,23},{8,24},{9,... | collective-permute-start | bytes 442376 | tf_op jit(solution)/shard_map/ppermute | solution.py:359
  6.8 9.0 %collective-permute-start.2 = (f32[3,24,512]{2,1,0:T(8,128)S(1)}, f32[3,24,512]{2,1,0:T(8,128)S(1)}, u32[]{:S(2)}, u32[]{:S(2)}) collective-permute-start(f32[3,24,512]{2,1,0:T(8,128)S(1)} %get-tuple-element.32), channel_id=1, source_target_pairs={{0,1},{1,0},{2,3},{3,2},{4,5},{5,4},{6,7},{7,6},{8,9},{9,8},{10,11... | collective-permute-start | bytes 442376 | tf_op jit(solution)/shard_map/ppermute | solution.py:359
  8.6 9.5 %collective-permute-start.3 = (f32[3,24,512]{2,1,0:T(8,128)S(1)}, f32[3,24,512]{2,1,0:T(8,128)S(1)}, u32[]{:S(2)}, u32[]{:S(2)}) collective-permute-start(f32[3,24,512]{2,1,0:T(8,128)S(1)} %get-tuple-element.33), channel_id=1, source_target_pairs={{0,17},{1,16},{2,19},{3,18},{4,21},{5,20},{6,23},{7,22},{8,25},{9,... | collective-permute-start | bytes 442376 | tf_op jit(solution)/shard_map/ppermute | solution.py:359
  18.3 5.9 %collective-permute-start.10 = (f32[3,3,24,512]{3,2,1,0:T(8,128)S(1)}, f32[3,3,24,512]{3,2,1,0:T(8,128)S(1)}, u32[]{:S(2)}, u32[]{:S(2)}) collective-permute-start(f32[3,3,24,512]{3,2,1,0:T(8,128)S(1)} %get-tuple-element.41), channel_id=1, source_target_pairs={{0,8},{1,9},{2,10},{3,11},{4,12},{5,13},{6,14},{7,15},{8,0},{9,1},... | collective-permute-start | bytes 1327112 | tf_op jit(solution)/shard_map/ppermute | solution.py:359
  19.8 9.6 %collective-permute-start.8 = (f32[3,2,24,512]{3,2,1,0:T(8,128)S(1)}, f32[3,2,24,512]{3,2,1,0:T(8,128)S(1)}, u32[]{:S(2)}, u32[]{:S(2)}) collective-permute-start(f32[3,2,24,512]{3,2,1,0:T(8,128)S(1)} %get-tuple-element.39), channel_id=1, source_target_pairs={{2,8},{3,9},{4,10},{5,11},{6,12},{7,13},{8,2},{9,3},{10,4},{11,5},... | collective-permute-start | bytes 884744 | tf_op jit(solution)/shard_map/ppermute | solution.py:359
  22.9 6.5 %collective-permute-start.9 = (f32[3,1,24,512]{3,2,1,0:T(8,128)S(1)}, f32[3,1,24,512]{3,2,1,0:T(8,128)S(1)}, u32[]{:S(2)}, u32[]{:S(2)}) collective-permute-start(f32[3,1,24,512]{3,2,1,0:T(8,128)S(1)} %get-tuple-element.40), channel_id=1, source_target_pairs={{0,2},{1,3},{2,4},{3,5},{4,6},{5,7},{10,8},{11,9},{12,10},{13,11},... | collective-permute-start | bytes 442376 | tf_op jit(solution)/shard_map/ppermute | solution.py:359
  31.9 9.5 %collective-permute-start.11 = (f32[3,16,512]{2,1,0:T(8,128)S(1)}, f32[3,16,512]{2,1,0:T(8,128)S(1)}, u32[]{:S(2)}, u32[]{:S(2)}) collective-permute-start(f32[3,16,512]{2,1,0:T(8,128)S(1)} %get-tuple-element.49), channel_id=1, source_target_pairs={{0,3},{1,2},{2,9},{3,8},{4,17},{5,16},{6,25},{7,24},{8,5},{9,4},{1... | collective-permute-start | bytes 294920 | tf_op jit(solution)/shard_map/ppermute | solution.py:359
  36.1 6.8 %collective-permute-start.12 = (f32[3,16,512]{2,1,0:T(8,128)S(1)}, f32[3,16,512]{2,1,0:T(8,128)S(1)}, u32[]{:S(2)}, u32[]{:S(2)}) collective-permute-start(f32[3,16,512]{2,1,0:T(8,128)S(1)} %get-tuple-element.50), channel_id=1, source_target_pairs={{0,1},{1,0},{2,11},{3,10},{4,19},{5,18},{6,27},{7,26},{8,7},{9,6},... | collective-permute-start | bytes 294920 | tf_op jit(solution)/shard_map/ppermute | solution.py:359
  36.1 6.8 %collective-permute-start.13 = (f32[3,16,512]{2,1,0:T(8,128)S(1)}, f32[3,16,512]{2,1,0:T(8,128)S(1)}, u32[]{:S(2)}, u32[]{:S(2)}) collective-permute-start(f32[3,16,512]{2,1,0:T(8,128)S(1)} %get-tuple-element.51), channel_id=1, source_target_pairs={{0,2},{1,3},{2,8},{3,9},{4,16},{5,17},{6,24},{7,25},{8,4},{9,5},{1... | collective-permute-start | bytes 294920 | tf_op jit(solution)/shard_map/ppermute | solution.py:359
  39.4 7.7 %collective-permute-start.14 = (f32[3,16,512]{2,1,0:T(8,128)S(1)}, f32[3,16,512]{2,1,0:T(8,128)S(1)}, u32[]{:S(2)}, u32[]{:S(2)}) collective-permute-start(f32[3,16,512]{2,1,0:T(8,128)S(1)} %get-tuple-element.52), channel_id=1, source_target_pairs={{0,0},{1,1},{2,10},{3,11},{4,18},{5,19},{6,26},{7,27},{8,6},{9,7},... | collective-permute-start | bytes 294920 | tf_op jit(solution)/shard_map/ppermute | solution.py:359
where the time goes:
time: 48.1 us; the launch traced here: 47.9 us
  starting transfers between devices  19.9 us (41%)
  waiting for transfers between devices  17.4 us (36%)
  Pallas kernels  8.34 us (17%)
  between operations  1.42 us (3%)
  local copies, waits for them, and re-layouts  0.84 us (2%)
    ppermute x15, starting transfers between devices, send(): return lax.ppermute(x, ('bin', 'slab'), pairs)  19.9 us
    ppermute x15, waiting for transfers between devices, send(): return lax.ppermute(x, ('bin', 'slab'), pairs)  17.4 us
    pallas_call x8, Pallas kernels, call(): pl.pallas_call(kernel, out_shape=shapes, in_specs=[pl.BlockSpec(memory_sp...  8.34 us
  transfers between devices with their start and end apart: 15, of which 9 were waited for; matrix products, arithmetic and copies ran while one was open for 2% of the time, Pallas kernels for 8%

commit v1 on v0

--- a/solution.py
+++ b/solution.py
@@ -312,12 +312,13 @@
     return (TWISTS >> (2 * (4 * core + plane // (slabs // 8)))) & 3
 
 
-def gather_kernel(rows, r0, r1, r2, r3, out, sem):
+def gather_kernel(rows, keys, *refs):
+    blocks, (out, sem) = refs[: len(keys)], refs[-2:]
     slabs = lax.axis_size("slab")
     z = lax.axis_index("bin") * slabs + lax.axis_index("slab")
     twist = twist_of(z // 4 % 2, z // 8, slabs)
     copies = []
-    for n, (t, ref) in enumerate(zip(ROUNDS, (r0, r1, r2, r3))):
+    for n, (t, ref) in enumerate(zip(keys, blocks)):
         at = pl.multiple_of((z % 4 ^ t ^ twist) * rows, 8)
         copies.append(pltpu.make_async_copy(ref, out.at[:, 0, pl.ds(at, rows), :], sem.at[n]))
         copies[-1].start()
@@ -424,11 +425,21 @@
         return where
 
     blocks = [send(block, owner(key)) for key, block in zip(ROUNDS, blocks)]
+    out = [(3, 1, total, lanes)]
+    early = call(
+        functools.partial(gather_kernel, rows, ROUNDS[:3]),
+        out,
+        blocks[:3],
+        scratch=[pltpu.SemaphoreType.DMA((3,))],
+        out_space=pl.ANY,
+    )
     return call(
-        functools.partial(gather_kernel, rows),
-        [(3, 1, total, lanes)],
-        blocks,
-        scratch=[pltpu.SemaphoreType.DMA((4,))],
+        functools.partial(gather_kernel, rows, ROUNDS[3:]),
+        out,
+        (blocks[3], *early),
+        [VMEM, pl.ANY],
+        [pltpu.SemaphoreType.DMA((1,))],
+        {1: 0},
         out_space=pl.ANY,
     )[0]
 

time: 48.1 us -> 48 us (level)
  waiting for transfers between devices: 17.4 us -> 16.7 us
  Pallas kernels: 8.34 us -> 8.94 us
    ppermute x15, waiting for transfers between devices: 17.4 us -> 16.7 us  [send(): return lax.ppermute(x, ('bin', 'slab'), pairs)]
    pallas_call x8 -> x9, Pallas kernels: 8.34 us -> 8.94 us  [call(): pl.pallas_call(kernel, out_shape=shapes, in_specs=[pl.BlockSpec(memory_sp...]
  transfers between devices with their start and end apart: 15 -> 15, of which waited for: 9 -> 9; matrix products, arithmetic and copies ran while one was open for 2% -> 2% of each run, Pallas kernels for 8% -> 9%
where the time goes in v1:
time: 48 us; the launch traced here: 47.8 us
  starting transfers between devices  19.9 us (41%)
  waiting for transfers between devices  16.7 us (35%)
  Pallas kernels  8.94 us (19%)
  between operations  1.43 us (3%)
  local copies, waits for them, and re-layouts  0.84 us (2%)
    ppermute x15, starting transfers between devices, send(): return lax.ppermute(x, ('bin', 'slab'), pairs)  19.9 us
    ppermute x15, waiting for transfers between devices, send(): return lax.ppermute(x, ('bin', 'slab'), pairs)  16.7 us
    pallas_call x9, Pallas kernels, call(): pl.pallas_call(kernel, out_shape=shapes, in_specs=[pl.BlockSpec(memory_sp...  8.94 us
  transfers between devices with their start and end apart: 15, of which 9 were waited for; matrix products, arithmetic and copies ran while one was open for 2% of the time, Pallas kernels for 9%

profile of v1, /device:TPU:7, one launch (start us, length us, event | category | flops | bytes accessed | tf_op | source)
XLA Modules:
  0.0 47.8 jit_solution(5573213016488758823)
XLA Ops:
  0.0 1.2 %shard_map.47 = (f32[2,64,512]{2,1,0:T(8,128)S(1)}, f32[2,64,512]{2,1,0:T(8,128)S(1)}) custom-call(f32[2,4,64,512]{3,2,1,0:T(8,128)} %volumes.5), custom_call_target="tpu_custom_call" | custom-call | bytes 1572880 | tf_op jit(solution)/shard_map/pallas_call | solution.py:333
  1.2 0.7 %collective-permute-start.4 = (f32[2,64,512]{2,1,0:T(8,128)S(1)}, f32[2,64,512]{2,1,0:T(8,128)S(1)}, u32[]{:S(2)}, u32[]{:S(2)}) collective-permute-start(f32[2,64,512]{2,1,0:T(8,128)S(1)} %get-tuple-element.34), channel_id=1, source_target_pairs={{0,8},{1,9},{2,10},{3,11},{4,12},{5,13},{6,14},{7,15},{8,0},{9,1},... | collective-permute-start | bytes 786440 | tf_op jit(solution)/shard_map/ppermute | solution.py:360
  2.0 0.8 %broadcast_in_dim.7 = f32[24]{0:T(128)S(1)} reshape(f32[3,8]{1,0:T(4,128)} %bitcast.1) | data formatting | bytes 192 | tf_op jit(solution)/shard_map/broadcast_in_dim | solution.py:363
  2.8 0.3 collective-permute-done.4.other
  3.9 2.3 %collective-permute-start.7 = (f32[3,24,512]{2,1,0:T(8,128)S(1)}, f32[3,24,512]{2,1,0:T(8,128)S(1)}, u32[]{:S(2)}, u32[]{:S(2)}) collective-permute-start(f32[3,24,512]{2,1,0:T(8,128)S(1)} %get-tuple-element.38), channel_id=1, source_target_pairs={{0,17},{1,16},{2,19},{3,18},{4,21},{5,20},{6,23},{7,22},{8,25},{9,... | collective-permute-start | bytes 442376 | tf_op jit(solution)/shard_map/ppermute | solution.py:360
  6.9 1.7 %collective-permute-done.5.refs_5_ = f32[3,24,512]{2,1,0:T(8,128)S(1)} collective-permute-done((f32[3,24,512]{2,1,0:T(8,128)S(1)}, f32[3,24,512]{2,1,0:T(8,128)S(1)}, u32[]{:S(2)}, u32[]{:S(2)}) %collective-permute-start.5) | collective-permute-done | bytes 147488 | tf_op jit(solution)/shard_map/ppermute | solution.py:360
  8.6 0.6 %collective-permute-start.3 = (f32[3,24,512]{2,1,0:T(8,128)S(1)}, f32[3,24,512]{2,1,0:T(8,128)S(1)}, u32[]{:S(2)}, u32[]{:S(2)}) collective-permute-start(f32[3,24,512]{2,1,0:T(8,128)S(1)} %get-tuple-element.33), channel_id=1, source_target_pairs={{0,17},{1,16},{2,19},{3,18},{4,21},{5,20},{6,23},{7,22},{8,25},{9,... | collective-permute-start | bytes 442376 | tf_op jit(solution)/shard_map/ppermute | solution.py:360
  10.6 1.1 %collective-permute-done.7.refs_7_ = f32[3,24,512]{2,1,0:T(8,128)S(1)} collective-permute-done((f32[3,24,512]{2,1,0:T(8,128)S(1)}, f32[3,24,512]{2,1,0:T(8,128)S(1)}, u32[]{:S(2)}, u32[]{:S(2)}) %collective-permute-start.7) | collective-permute-done | bytes 147488 | tf_op jit(solution)/shard_map/ppermute | solution.py:360
  11.8 3.2 %collective-permute-done.1.refs_1_ = f32[3,24,512]{2,1,0:T(8,128)S(1)} collective-permute-done((f32[3,24,512]{2,1,0:T(8,128)S(1)}, f32[3,24,512]{2,1,0:T(8,128)S(1)}, u32[]{:S(2)}, u32[]{:S(2)}) %collective-permute-start.1) | collective-permute-done | bytes 147488 | tf_op jit(solution)/shard_map/ppermute | solution.py:360
  15.0 0.8 %collective-permute-done.2.refs_2_ = f32[3,24,512]{2,1,0:T(8,128)S(1)} collective-permute-done((f32[3,24,512]{2,1,0:T(8,128)S(1)}, f32[3,24,512]{2,1,0:T(8,128)S(1)}, u32[]{:S(2)}, u32[]{:S(2)}) %collective-permute-start.2) | collective-permute-done | bytes 147488 | tf_op jit(solution)/shard_map/ppermute | solution.py:360
  15.8 2.3 %collective-permute-done.3.refs_3_ = f32[3,24,512]{2,1,0:T(8,128)S(1)} collective-permute-done((f32[3,24,512]{2,1,0:T(8,128)S(1)}, f32[3,24,512]{2,1,0:T(8,128)S(1)}, u32[]{:S(2)}, u32[]{:S(2)}) %collective-permute-start.3) | collective-permute-done | bytes 147488 | tf_op jit(solution)/shard_map/ppermute | solution.py:360
  18.3 1.5 %collective-permute-start.10 = (f32[3,3,24,512]{3,2,1,0:T(8,128)S(1)}, f32[3,3,24,512]{3,2,1,0:T(8,128)S(1)}, u32[]{:S(2)}, u32[]{:S(2)}) collective-permute-start(f32[3,3,24,512]{3,2,1,0:T(8,128)S(1)} %get-tuple-element.41), channel_id=1, source_target_pairs={{0,8},{1,9},{2,10},{3,11},{4,12},{5,13},{6,14},{7,15},{8,0},{9,1},... | collective-permute-start | bytes 1327112 | tf_op jit(solution)/shard_map/ppermute | solution.py:360
  19.8 3.1 %collective-permute-start.8 = (f32[3,2,24,512]{3,2,1,0:T(8,128)S(1)}, f32[3,2,24,512]{3,2,1,0:T(8,128)S(1)}, u32[]{:S(2)}, u32[]{:S(2)}) collective-permute-start(f32[3,2,24,512]{3,2,1,0:T(8,128)S(1)} %get-tuple-element.39), channel_id=1, source_target_pairs={{2,8},{3,9},{4,10},{5,11},{6,12},{7,13},{8,2},{9,3},{10,4},{11,5},... | collective-permute-start | bytes 884744 | tf_op jit(solution)/shard_map/ppermute | solution.py:360
  22.9 1.3 %collective-permute-start.9 = (f32[3,1,24,512]{3,2,1,0:T(8,128)S(1)}, f32[3,1,24,512]{3,2,1,0:T(8,128)S(1)}, u32[]{:S(2)}, u32[]{:S(2)}) collective-permute-start(f32[3,1,24,512]{3,2,1,0:T(8,128)S(1)} %get-tuple-element.40), channel_id=1, source_target_pairs={{0,2},{1,3},{2,4},{3,5},{4,6},{5,7},{10,8},{11,9},{12,10},{13,11},... | collective-permute-start | bytes 442376 | tf_op jit(solution)/shard_map/ppermute | solution.py:360
  24.3 3.1 %shard_map.51 = (f32[3,10,24,512]{3,2,1,0:T(8,128)S(1)}, f32[3,10,24,512]{3,2,1,0:T(8,128)S(1)}, f32[3,10,24,512]{3,2,1,0:T(8,128)S(1)}, f32[3,5,24,512]{3,2,1,0...) custom-call(f32[19,8,128]{2,1,0:T(8,128)S(1)} %shard_map.46.numbers, ...), custom_call_target="tpu_custom_call", output_to_operand_aliasing={{0}: (2, {})} | custom-call | flops 22118400 | bytes 11726848 | tf_op jit(solution)/shard_map/pallas_call | solution.py:333
  27.4 2.1 %collective-permute-done.9.near = f32[3,1,24,512]{3,2,1,0:T(8,128)S(1)} collective-permute-done((f32[3,1,24,512]{3,2,1,0:T(8,128)S(1)}, f32[3,1,24,512]{3,2,1,0:T(8,128)S(1)}, u32[]{:S(2)}, u32[]{:S(2)}) %collective-permute-start.9) | collective-permute-done | bytes 147488 | tf_op jit(solution)/shard_map/ppermute | solution.py:360
  29.4 2.4 %shard_map.52 = (f32[3,10,24,512]{3,2,1,0:T(8,128)S(1)}, f32[3,10,24,512]{3,2,1,0:T(8,128)S(1)}, f32[3,10,24,512]{3,2,1,0:T(8,128)S(1)}, f32[3,5,24,512]{3,2,1,0...) custom-call(f32[19,8,128]{2,1,0:T(8,128)S(1)} %shard_map.46.numbers,, ...), custom_call_target="tpu_custom_call", output_to_operand_aliasing={{0}: (3, {}), {1}: (4, {}), {2}: (5, {}), {3}: (6, {}), {4}... | custom-call | flops 16588800 | bytes 19787776 | tf_op jit(solution)/shard_map/pallas_call | solution.py:333
  31.9 4.3 %collective-permute-start.12 = (f32[3,16,512]{2,1,0:T(8,128)S(1)}, f32[3,16,512]{2,1,0:T(8,128)S(1)}, u32[]{:S(2)}, u32[]{:S(2)}) collective-permute-start(f32[3,16,512]{2,1,0:T(8,128)S(1)} %get-tuple-element.50), channel_id=1, source_target_pairs={{0,3},{1,2},{2,9},{3,8},{4,17},{5,16},{6,25},{7,24},{8,5},{9,4},{1... | collective-permute-start | bytes 294920 | tf_op jit(solution)/shard_map/ppermute | solution.py:360
  36.1 3.3 %collective-permute-start.14 = (f32[3,16,512]{2,1,0:T(8,128)S(1)}, f32[3,16,512]{2,1,0:T(8,128)S(1)}, u32[]{:S(2)}, u32[]{:S(2)}) collective-permute-start(f32[3,16,512]{2,1,0:T(8,128)S(1)} %get-tuple-element.52), channel_id=1, source_target_pairs={{0,2},{1,3},{2,8},{3,9},{4,16},{5,17},{6,24},{7,25},{8,4},{9,5},{1... | collective-permute-start | bytes 294920 | tf_op jit(solution)/shard_map/ppermute | solution.py:360
  39.4 1.9 %collective-permute-start.11 = (f32[3,16,512]{2,1,0:T(8,128)S(1)}, f32[3,16,512]{2,1,0:T(8,128)S(1)}, u32[]{:S(2)}, u32[]{:S(2)}) collective-permute-start(f32[3,16,512]{2,1,0:T(8,128)S(1)} %get-tuple-element.49), channel_id=1, source_target_pairs={{0,0},{1,1},{2,10},{3,11},{4,18},{5,19},{6,26},{7,27},{8,6},{9,7},... | collective-permute-start | bytes 294920 | tf_op jit(solution)/shard_map/ppermute | solution.py:360
  41.3 1.6 %collective-permute-done.13.refs_1_ = f32[3,16,512]{2,1,0:T(8,128)S(1)} collective-permute-done((f32[3,16,512]{2,1,0:T(8,128)S(1)}, f32[3,16,512]{2,1,0:T(8,128)S(1)}, u32[]{:S(2)}, u32[]{:S(2)}) %collective-permute-start.13) | collective-permute-done | bytes 98336 | tf_op jit(solution)/shard_map/ppermute | solution.py:360
  42.9 0.7 %shard_map.53.refs_1_ = f32[3,1,64,512]{3,2,1,0:T(8,128)} custom-call(f32[3,16,512]{2,1,0:T(8,128)S(1)} %collective-permute-done.12.refs_0_, f32[3,16,512]{2,1,0:T(8,128)S(1)} %collective-permute-done.13.refs_1_, f32[3,16,512]{2,1,0:T(8,128)S(1)} %collective-permute-done.14.refs_2_), custom_call_target="tpu_custom_call" | custom-call | bytes 688140 | tf_op jit(solution)/shard_map/pallas_call | solution.py:333
  43.7 3.5 %collective-permute-done.11.refs_0_ = f32[3,16,512]{2,1,0:T(8,128)S(1)} collective-permute-done((f32[3,16,512]{2,1,0:T(8,128)S(1)}, f32[3,16,512]{2,1,0:T(8,128)S(1)}, u32[]{:S(2)}, u32[]{:S(2)}) %collective-permute-start.11) | collective-permute-done | bytes 98336 | tf_op jit(solution)/shard_map/ppermute | solution.py:360
  47.1 0.6 %shard_map.54 = f32[3,1,64,512]{3,2,1,0:T(8,128)} custom-call(f32[3,16,512]{2,1,0:T(8,128)S(1)} %collective-permute-done.11.refs_0_, f32[3,1,64,512]{3,2,1,0:T(8,128)} %shard_map.53.refs_1_), custom_call_target="tpu_custom_call", output_to_operand_aliasing={{}: (1, {})} | custom-call | bytes 884740 | tf_op jit(solution)/shard_map/pallas_call | solution.py:333
  (19 shorter events, 1.7 us)
Async XLA Ops:
  0.0 3.2 %copy-start = (f32[2,4,64,512]{3,2,1,0:T(8,128)S(1)}, f32[2,4,64,512]{3,2,1,0:T(8,128)}, u32[]{:S(2)}) copy-start(f32[2,4,64,512]{3,2,1,0:T(8,128)} %volumes.5) | copy-start | bytes 3145732
  1.2 1.9 %collective-permute-start.4 = (f32[2,64,512]{2,1,0:T(8,128)S(1)}, f32[2,64,512]{2,1,0:T(8,128)S(1)}, u32[]{:S(2)}, u32[]{:S(2)}) collective-permute-start(f32[2,64,512]{2,1,0:T(8,128)S(1)} %get-tuple-element.34), channel_id=1, source_target_pairs={{0,8},{1,9},{2,10},{3,11},{4,12},{5,13},{6,14},{7,15},{8,0},{9,1},... | collective-permute-start | bytes 786440 | tf_op jit(solution)/shard_map/ppermute | solution.py:360
  2.0 4.3 %collective-permute-start = (f32[2,64,512]{2,1,0:T(8,128)S(1)}, f32[2,64,512]{2,1,0:T(8,128)S(1)}, u32[]{:S(2)}, u32[]{:S(2)}) collective-permute-start(f32[2,64,512]{2,1,0:T(8,128)S(1)} %get-tuple-element.29), channel_id=1, source_target_pairs={{0,8},{1,9},{2,10},{3,11},{4,12},{5,13},{6,14},{7,15},{8,0},{9,1},... | collective-permute-start | bytes 786440 | tf_op jit(solution)/shard_map/ppermute | solution.py:360
  3.5 5.1 %collective-permute-start.5 = (f32[3,24,512]{2,1,0:T(8,128)S(1)}, f32[3,24,512]{2,1,0:T(8,128)S(1)}, u32[]{:S(2)}, u32[]{:S(2)}) collective-permute-start(f32[3,24,512]{2,1,0:T(8,128)S(1)} %get-tuple-element.36), channel_id=1, source_target_pairs={{0,16},{1,17},{2,18},{3,19},{4,20},{5,21},{6,22},{7,23},{8,24},{9,... | collective-permute-start | bytes 442376 | tf_op jit(solution)/shard_map/ppermute | solution.py:360
  3.8 6.8 %collective-permute-start.6 = (f32[3,24,512]{2,1,0:T(8,128)S(1)}, f32[3,24,512]{2,1,0:T(8,128)S(1)}, u32[]{:S(2)}, u32[]{:S(2)}) collective-permute-start(f32[3,24,512]{2,1,0:T(8,128)S(1)} %get-tuple-element.37), channel_id=1, source_target_pairs={{0,1},{1,0},{2,3},{3,2},{4,5},{5,4},{6,7},{7,6},{8,9},{9,8},{10,11... | collective-permute-start | bytes 442376 | tf_op jit(solution)/shard_map/ppermute | solution.py:360
  3.9 7.9 %collective-permute-start.7 = (f32[3,24,512]{2,1,0:T(8,128)S(1)}, f32[3,24,512]{2,1,0:T(8,128)S(1)}, u32[]{:S(2)}, u32[]{:S(2)}) collective-permute-start(f32[3,24,512]{2,1,0:T(8,128)S(1)} %get-tuple-element.38), channel_id=1, source_target_pairs={{0,17},{1,16},{2,19},{3,18},{4,21},{5,20},{6,23},{7,22},{8,25},{9,... | collective-permute-start | bytes 442376 | tf_op jit(solution)/shard_map/ppermute | solution.py:360
  6.5 8.5 %collective-permute-start.1 = (f32[3,24,512]{2,1,0:T(8,128)S(1)}, f32[3,24,512]{2,1,0:T(8,128)S(1)}, u32[]{:S(2)}, u32[]{:S(2)}) collective-permute-start(f32[3,24,512]{2,1,0:T(8,128)S(1)} %get-tuple-element.31), channel_id=1, source_target_pairs={{0,16},{1,17},{2,18},{3,19},{4,20},{5,21},{6,22},{7,23},{8,24},{9,... | collective-permute-start | bytes 442376 | tf_op jit(solution)/shard_map/ppermute | solution.py:360
  6.8 9.0 %collective-permute-start.2 = (f32[3,24,512]{2,1,0:T(8,128)S(1)}, f32[3,24,512]{2,1,0:T(8,128)S(1)}, u32[]{:S(2)}, u32[]{:S(2)}) collective-permute-start(f32[3,24,512]{2,1,0:T(8,128)S(1)} %get-tuple-element.32), channel_id=1, source_target_pairs={{0,1},{1,0},{2,3},{3,2},{4,5},{5,4},{6,7},{7,6},{8,9},{9,8},{10,11... | collective-permute-start | bytes 442376 | tf_op jit(solution)/shard_map/ppermute | solution.py:360
  8.6 9.5 %collective-permute-start.3 = (f32[3,24,512]{2,1,0:T(8,128)S(1)}, f32[3,24,512]{2,1,0:T(8,128)S(1)}, u32[]{:S(2)}, u32[]{:S(2)}) collective-permute-start(f32[3,24,512]{2,1,0:T(8,128)S(1)} %get-tuple-element.33), channel_id=1, source_target_pairs={{0,17},{1,16},{2,19},{3,18},{4,21},{5,20},{6,23},{7,22},{8,25},{9,... | collective-permute-start | bytes 442376 | tf_op jit(solution)/shard_map/ppermute | solution.py:360
  18.3 5.9 %collective-permute-start.10 = (f32[3,3,24,512]{3,2,1,0:T(8,128)S(1)}, f32[3,3,24,512]{3,2,1,0:T(8,128)S(1)}, u32[]{:S(2)}, u32[]{:S(2)}) collective-permute-start(f32[3,3,24,512]{3,2,1,0:T(8,128)S(1)} %get-tuple-element.41), channel_id=1, source_target_pairs={{0,8},{1,9},{2,10},{3,11},{4,12},{5,13},{6,14},{7,15},{8,0},{9,1},... | collective-permute-start | bytes 1327112 | tf_op jit(solution)/shard_map/ppermute | solution.py:360
  19.8 9.6 %collective-permute-start.8 = (f32[3,2,24,512]{3,2,1,0:T(8,128)S(1)}, f32[3,2,24,512]{3,2,1,0:T(8,128)S(1)}, u32[]{:S(2)}, u32[]{:S(2)}) collective-permute-start(f32[3,2,24,512]{3,2,1,0:T(8,128)S(1)} %get-tuple-element.39), channel_id=1, source_target_pairs={{2,8},{3,9},{4,10},{5,11},{6,12},{7,13},{8,2},{9,3},{10,4},{11,5},... | collective-permute-start | bytes 884744 | tf_op jit(solution)/shard_map/ppermute | solution.py:360
  22.9 6.5 %collective-permute-start.9 = (f32[3,1,24,512]{3,2,1,0:T(8,128)S(1)}, f32[3,1,24,512]{3,2,1,0:T(8,128)S(1)}, u32[]{:S(2)}, u32[]{:S(2)}) collective-permute-start(f32[3,1,24,512]{3,2,1,0:T(8,128)S(1)} %get-tuple-element.40), channel_id=1, source_target_pairs={{0,2},{1,3},{2,4},{3,5},{4,6},{5,7},{10,8},{11,9},{12,10},{13,11},... | collective-permute-start | bytes 442376 | tf_op jit(solution)/shard_map/ppermute | solution.py:360
  31.9 9.5 %collective-permute-start.12 = (f32[3,16,512]{2,1,0:T(8,128)S(1)}, f32[3,16,512]{2,1,0:T(8,128)S(1)}, u32[]{:S(2)}, u32[]{:S(2)}) collective-permute-start(f32[3,16,512]{2,1,0:T(8,128)S(1)} %get-tuple-element.50), channel_id=1, source_target_pairs={{0,3},{1,2},{2,9},{3,8},{4,17},{5,16},{6,25},{7,24},{8,5},{9,4},{1... | collective-permute-start | bytes 294920 | tf_op jit(solution)/shard_map/ppermute | solution.py:360
  36.1 6.8 %collective-permute-start.13 = (f32[3,16,512]{2,1,0:T(8,128)S(1)}, f32[3,16,512]{2,1,0:T(8,128)S(1)}, u32[]{:S(2)}, u32[]{:S(2)}) collective-permute-start(f32[3,16,512]{2,1,0:T(8,128)S(1)} %get-tuple-element.51), channel_id=1, source_target_pairs={{0,1},{1,0},{2,11},{3,10},{4,19},{5,18},{6,27},{7,26},{8,7},{9,6},... | collective-permute-start | bytes 294920 | tf_op jit(solution)/shard_map/ppermute | solution.py:360
  36.1 6.8 %collective-permute-start.14 = (f32[3,16,512]{2,1,0:T(8,128)S(1)}, f32[3,16,512]{2,1,0:T(8,128)S(1)}, u32[]{:S(2)}, u32[]{:S(2)}) collective-permute-start(f32[3,16,512]{2,1,0:T(8,128)S(1)} %get-tuple-element.52), channel_id=1, source_target_pairs={{0,2},{1,3},{2,8},{3,9},{4,16},{5,17},{6,24},{7,25},{8,4},{9,5},{1... | collective-permute-start | bytes 294920 | tf_op jit(solution)/shard_map/ppermute | solution.py:360
  39.4 7.7 %collective-permute-start.11 = (f32[3,16,512]{2,1,0:T(8,128)S(1)}, f32[3,16,512]{2,1,0:T(8,128)S(1)}, u32[]{:S(2)}, u32[]{:S(2)}) collective-permute-start(f32[3,16,512]{2,1,0:T(8,128)S(1)} %get-tuple-element.49), channel_id=1, source_target_pairs={{0,0},{1,1},{2,10},{3,11},{4,18},{5,19},{6,26},{7,27},{8,6},{9,7},... | collective-permute-start | bytes 294920 | tf_op jit(solution)/shard_map/ppermute | solution.py:360
